TPU v7x, 32 devices: a whole 2x2x4 slice. The times are simulated.
32 devices in a mesh: gx: 4 (over y, x), gy: 8 (over z, core).
Axes of the slice: x: 2, y: 2, z: 4, core: 2. Of those that a mesh axis runs over, the one named last changes fastest.
Arguments:
- inputs: bfloat16 [16, 16, 32, 512], P('gx', 'gy'), may hold values from -6 to 6
- cotangent: bfloat16 [16, 16, 32, 512], P('gx', 'gy'), may hold values from -6 to 6
- point_weight: bfloat16 [32, 32], replicated, may hold values from -1 to 1
- spectral_weight: bfloat16 [2304, 24, 2048], P(('gx', 'gy')), may hold values from -0.75 to 0.75
Outputs:
- grad_input: bfloat16 [16, 16, 32, 512], P('gx', 'gy')
- grad_spectral: float32 [2304, 24, 2048], P(('gx', 'gy'))
All inputs are finite; a program needn't handle non-finite values.
Results may differ from a plain program's by a relative error of at most 0.034.
Values may be sent and summed in bfloat16 or wider, within the bound.
No kernel may reach another device: no remote copies, remote signals or barrier semaphores. Data moves between devices by JAX's collectives and lax.ppermute only.
A program may use at most 192 MiB of HBM per device.

v0:
```python
import math
import jax
import jax.numpy as jnp
from jax import lax
from jax.sharding import PartitionSpec as P

NZ = 64
NT = 8
KX = 24
KY = 24
KZ = 12
KT = 8


def kept_angles(positions, kept_count, length):
    index = jnp.arange(kept_count, dtype=jnp.int32)
    frequency = jnp.where(index < kept_count // 2, index, index - kept_count)
    turns = positions[:, None] * frequency[None, :] % length
    return turns.astype(jnp.float32) * (2.0 * math.pi / length)


def axis_tables(positions, kept_count, length):
    angles = kept_angles(positions, kept_count, length)
    return (jnp.cos(angles), jnp.sin(angles))


def depth_tables():
    angle_depth = kept_angles(jnp.arange(NZ, dtype=jnp.int32), KZ, NZ)
    angle_time = kept_angles(jnp.arange(NT, dtype=jnp.int32), KT, NT)
    angles = (angle_depth[:, None, :, None] + angle_time[None, :, None, :]).reshape(
        NZ * NT, KZ * KT
    )
    return (jnp.cos(angles), jnp.sin(angles))


def settle(values):
    return lax.optimization_barrier(values.astype(jnp.bfloat16))


def rotate(spectra, cosine_table, sine_table, pattern, turn_sign):
    half_width = spectra.shape[-1] // 2
    with_cosine = jnp.einsum(pattern, spectra, cosine_table, precision=lax.Precision.HIGHEST)
    with_sine = jnp.einsum(pattern, spectra, sine_table, precision=lax.Precision.HIGHEST)
    real_part = with_cosine[..., :half_width] + turn_sign * with_sine[..., half_width:]
    imag_part = with_cosine[..., half_width:] - turn_sign * with_sine[..., :half_width]
    return jnp.concatenate([real_part, imag_part], -1)


def depth_forward(field_in, tables, factor):
    widened = field_in.astype(jnp.float32)
    with_cosine = jnp.einsum("xycs,sk->kxyc", widened, tables[0], precision=lax.Precision.HIGHEST)
    with_sine = jnp.einsum("xycs,sk->kxyc", widened, tables[1], precision=lax.Precision.HIGHEST)
    return jnp.concatenate([with_cosine, -with_sine], -1) * factor


def depth_inverse(spectra, tables, factor):
    half_width = spectra.shape[-1] // 2
    with_cosine = jnp.einsum(
        "kxyc,sk->xycs", spectra[..., :half_width], tables[0], precision=lax.Precision.HIGHEST
    )
    with_sine = jnp.einsum(
        "kxyc,sk->xycs", spectra[..., half_width:], tables[1], precision=lax.Precision.HIGHEST
    )
    return (with_cosine - with_sine) * factor


def contract_in(left, right):
    return jnp.einsum("mkc,mkco->mko", left, right, precision=lax.Precision.HIGHEST)


def contract_out(left, right):
    return jnp.einsum("mko,mkco->mkc", left, right, precision=lax.Precision.HIGHEST)


def partial_outer(left, right):
    return jnp.einsum("mkc,mko->mkco", left, right, precision=lax.Precision.HIGHEST)


def mix_modes(spectra, weight):
    half_width = spectra.shape[-1] // 2
    weight_wide = weight.astype(jnp.float32)
    weight_real, weight_imag = (weight_wide[..., :half_width], weight_wide[..., half_width:])
    real_in, imag_in = (spectra[..., :half_width], spectra[..., half_width:])
    real_out = contract_in(real_in, weight_real) - contract_in(imag_in, weight_imag)
    imag_out = contract_in(real_in, weight_imag) + contract_in(imag_in, weight_real)
    return jnp.concatenate([real_out, imag_out], -1)


def adjoint_modes(spectra, weight):
    half_width = spectra.shape[-1] // 2
    weight_wide = weight.astype(jnp.float32)
    weight_real, weight_imag = (weight_wide[..., :half_width], weight_wide[..., half_width:])
    real_in, imag_in = (spectra[..., :half_width], spectra[..., half_width:])
    real_out = contract_out(real_in, weight_real) + contract_out(imag_in, weight_imag)
    imag_out = contract_out(imag_in, weight_real) - contract_out(real_in, weight_imag)
    return jnp.concatenate([real_out, imag_out], -1)


def weight_grad(spectra_in, spectra_back):
    half_width = spectra_in.shape[-1] // 2
    real_in, imag_in = (spectra_in[..., :half_width], spectra_in[..., half_width:])
    real_back, imag_back = (spectra_back[..., :half_width], spectra_back[..., half_width:])
    real_part = partial_outer(real_in, real_back) + partial_outer(imag_in, imag_back)
    imag_part = partial_outer(real_in, imag_back) - partial_outer(imag_in, real_back)
    return jnp.concatenate([real_part, imag_part], -1)


def exact_gelu(values):
    return jax.nn.gelu(values, approximate=False)


def per_device(inputs, cotangent, point_weight, spectral_weight):
    rows_x, rows_y, channels, cells = inputs.shape
    mode_rows, mode_cols, flat_width = spectral_weight.shape
    weight_blocks = spectral_weight.reshape(mode_rows, mode_cols, channels, 2 * channels)
    count_gx = lax.axis_size("gx")
    count_gy = lax.axis_size("gy")
    length_x = rows_x * count_gx
    length_y = rows_y * count_gy
    depth_pair = depth_tables()
    own_x = lax.axis_index("gx") * rows_x + jnp.arange(rows_x, dtype=jnp.int32)
    local_x = axis_tables(own_x, KX, length_x)
    whole_y = axis_tables(jnp.arange(length_y, dtype=jnp.int32), KY, length_y)
    total_cells = length_x * length_y * cells
    kept_total = KX * KY * KZ * KT

    def to_modes(field_in, factor):
        depth_spec = settle(depth_forward(field_in, depth_pair, factor))
        share = depth_spec.shape[0] // count_gx
        first_spectra = lax.psum_scatter(
            rotate(
                depth_spec.astype(jnp.float32), local_x[0], local_x[1], "rxyc,xk->rkyc", 1.0
            ).astype(jnp.bfloat16),
            "gx",
            scatter_dimension=0,
            tiled=True,
        ).astype(jnp.float32)
        first_spectra = settle(first_spectra).reshape(share * KX, rows_y, 2 * channels)
        arrived_modes = lax.all_to_all(first_spectra, "gy", split_axis=0, concat_axis=1, tiled=True)
        return rotate(arrived_modes.astype(jnp.float32), whole_y[0], whole_y[1], "myc,yk->mkc", 1.0)

    def to_space(spectra, factor):
        back_rows = settle(rotate(spectra, whole_y[0], whole_y[1], "mkc,yk->myc", -1.0))
        returned = lax.all_to_all(back_rows, "gy", split_axis=1, concat_axis=0, tiled=True)
        share = returned.shape[0] // KX
        returned = returned.reshape(share, KX, rows_y, 2 * channels)
        back_depth = settle(
            rotate(
                lax.all_gather(returned, "gx", axis=0, tiled=True).astype(jnp.float32),
                local_x[0],
                local_x[1],
                "rkyc,xk->rxyc",
                -1.0,
            )
        )
        return depth_inverse(back_depth.astype(jnp.float32), depth_pair, factor)

    spectra_in = to_modes(inputs, 1.0 / math.sqrt(total_cells))
    mixed = mix_modes(spectra_in, weight_blocks)
    spectral_out = to_space(mixed, 1.0 / math.sqrt(kept_total))
    pointwise = jnp.einsum(
        "xycs,co->xyos", inputs, point_weight, preferred_element_type=jnp.float32
    )
    before = spectral_out + pointwise
    unused_out, pullback = jax.vjp(exact_gelu, before)
    slope = settle(pullback(cotangent.astype(jnp.float32))[0])
    spectra_back = to_modes(slope, 1.0 / math.sqrt(kept_total))
    grad_spectral = weight_grad(spectra_in, spectra_back).reshape(mode_rows, mode_cols, flat_width)
    adjoint = adjoint_modes(spectra_back, weight_blocks)
    spectral_grad = to_space(adjoint, 1.0 / math.sqrt(total_cells))
    pointwise_grad = jnp.einsum(
        "xyos,co->xycs", slope, point_weight, preferred_element_type=jnp.float32
    )
    grad_input = (pointwise_grad + spectral_grad).astype(jnp.bfloat16)
    return (grad_input, grad_spectral)


def solution(mesh):
    placed = (
        P("gx", "gy", None, None),
        P("gx", "gy", None, None),
        P(),
        P(("gx", "gy"), None, None),
    )
    return jax.shard_map(
        per_device,
        mesh=mesh,
        in_specs=placed,
        out_specs=(P("gx", "gy", None, None), P(("gx", "gy"), None, None)),
        check_vma=False,
    )
```

profile of v0, /device:TPU:0, one launch (start us, length us, event | category | flops | bytes accessed | tf_op | source)
XLA Modules:
  0.0 453.6 jit_solution(6818993007358127799)
XLA Ops:
  7.4 12.3 %add_sine_fusion = (f32[64,8,12,8]{1,0,3,2:T(8,128)}, f32[64,8,12,8]{1,0,3,2:T(8,128)S(1)}) fusion(f32[8,8]{0,1:T(8,128)S(1)} %fusion.94, f32[64,12]{0,1:T(8,128)S(1)} %fusion.75), kind=kLoop, calls=%fused_computation.19 | loop fusion | flops 49152 | bytes 396544 | tf_op jit(solution)/shard_map/sin | solution.py:33
  19.8 3.9 reshape.129
  23.7 2.8 reshape.128
  33.1 31.4 %reduce-scatter.3.cloned.1.call-done = bf16[24,24,2,64]{3,1,2,0:T(8,128)(2,1)} async-done(((bf16[96,24,2,64]{3,1,2,0:T(8,128)(2,1)}), bf16[24,24,2,64]{3,1,2,0:T(8,128)(2,1)}) %reduce-scatter.3.cloned.1.call-update) | async-done | bytes 147472 | tf_op jit(solution)/shard_map/reduce_scatter | solution.py:130
  66.7 4.6 %all-to-all-start = ((bf16[8,2,4608]{2,1,0:T(2,128)(2,1)}), bf16[8,2,4608]{2,1,0:T(2,128)(2,1)S(1)}, u32[]{:S(2)}, u32[]{:S(2)}) async-start(bf16[8,2,4608]{2,1,0:T(2,128)(2,1)} %reshape.154), calls=%async_computation.1 | async-start | bytes 294912 | tf_op jit(solution)/shard_map/all_to_all | solution.py:139
  71.8 20.8 %reshape.123 = bf16[72,24,32,64]{3,2,1,0:T(8,128)(2,1)} reshape(bf16[72,24,2048]{2,1,0:T(8,128)(2,1)} %param.7) | data formatting | bytes 14155776 | tf_op jit(solution)/shard_map/reshape | solution.py:115
  95.3 34.3 %fusion.2 = (f32[72,24,32]{2,1,0:T(8,128)}, f32[72,24,32]{2,1,0:T(8,128)}, f32[72,24,32]{2,1,0:T(8,128)}, f32[72,24,32]{2,1,0:T(8,128)S(1)}) fusion(f32[72,24,32]{2,1,0:T(8,128)S(1)} %copy.146, bf16[72,24,32,64]{3,2,1,0:T(8,128)(2,1)} %reshape.123, f32[72,24,32]{2,1,0:T(8,128)S(1)} %copy.145), kind=kLoop, calls=%fused_computation.10 | loop fusion | flops 17473536 | bytes 8404992
  129.7 2.3 copy.111
  141.1 14.6 %all_to_all.66 = bf16[72,16,64]{0,2,1:T(8,128)(2,1)S(1)} all-to-all(bf16[72,16,64]{0,2,1:T(8,128)(2,1)S(1)} %copy.78), channel_id=1, replica_groups=mesh['gx'=4,'gy'=8] {'gy'}, dimensions={1} | all-to-all | bytes 294912 | tf_op jit(solution)/shard_map/all_to_all | solution.py:144
  158.0 38.1 %all_gather.6 = bf16[96,24,2,64]{1,0,3,2:T(8,128)(2,1)S(1)} all-gather(bf16[24,24,2,64]{1,0,3,2:T(8,128)(2,1)S(1)} %copy.80), channel_id=1, replica_groups=mesh['gx'=4,'gy'=8] {'gx'}, dimensions={0}, use_global_device_ids=true | all-gather | bytes 737280 | tf_op jit(solution)/shard_map/all_gather | solution.py:149
  196.1 5.8 %convolution_bitcast_fusion.16 = f32[96,4,2,64]{0,1,3,2:T(4,128)S(1)} fusion(bf16[96,24,2,64]{1,0,3,2:T(8,128)(2,1)S(1)} %all_gather.6, s32[24]{0:T(128)S(1)} %compare_select_fusion.2, s32[4]{0:T(128)S(1)} %iota_add_fusion), kind=kOutput, calls=%fused_computation.44 | convolution fusion | flops 14157120 | bytes 786544 | tf_op jit(solution)/shard_map/rkyc,xk->rxyc/dot_general | solution.py:43
  201.9 5.8 %convolution_bitcast_fusion.17 = f32[96,4,2,64]{0,1,3,2:T(4,128)S(1)} fusion(bf16[96,24,2,64]{1,0,3,2:T(8,128)(2,1)S(1)} %all_gather.6, s32[24]{0:T(128)S(1)} %compare_select_fusion.2, s32[4]{0:T(128)S(1)} %iota_add_fusion), kind=kOutput, calls=%fused_computation.45 | convolution fusion | flops 14157120 | bytes 786544 | tf_op jit(solution)/shard_map/rkyc,xk->rxyc/dot_general | solution.py:42
  208.9 2.4 fusion.22
  216.1 27.9 %reduce-scatter.5.cloned.1.call-done = bf16[24,24,2,64]{3,1,2,0:T(8,128)(2,1)} async-done(((bf16[96,24,2,64]{3,1,2,0:T(8,128)(2,1)}), bf16[24,24,2,64]{3,1,2,0:T(8,128)(2,1)}) %reduce-scatter.5.cloned.1.call-update) | async-done | bytes 147472 | tf_op jit(solution)/shard_map/reduce_scatter | solution.py:130
  245.5 11.6 %all_to_all.67 = bf16[8,2,4608]{2,1,0:T(2,128)(2,1)S(1)} all-to-all(bf16[8,2,4608]{2,1,0:T(2,128)(2,1)S(1)} %reshape.156), channel_id=1, replica_groups=mesh['gx'=4,'gy'=8] {'gy'}, dimensions={0} | all-to-all | bytes 294912 | tf_op jit(solution)/shard_map/all_to_all | solution.py:139
  261.3 2.3 copy.148
  263.6 38.7 %fusion.6 = (f32[72,24,32]{2,1,0:T(8,128)}, f32[72,24,32]{2,1,0:T(8,128)}, f32[72,24,32]{2,1,0:T(8,128)}, f32[72,24,32]{2,1,0:T(8,128)}) fusion(f32[72,24,32]{2,1,0:T(8,128)} %copy.148, bf16[72,24,32,64]{3,2,1,0:T(8,128)(2,1)} %reshape.123, f32[72,24,32]{2,1,0:T(8,128)S(1)} %copy.147), kind=kLoop, calls=%fused_computation.14 | loop fusion | flops 17473536 | bytes 8404992
  314.6 20.0 %multiply_add_fusion = (f32[72,24,32,32]{3,2,1,0:T(8,128)}, f32[72,24,32,32]{3,2,1,0:T(8,128)}) fusion(f32[72,24,32]{2,1,0:T(8,128)S(1)} %copy.146, f32[72,24,32]{2,1,0:T(8,128)S(1)} %copy.145, f32[72,24,32]{2,1,0:T(8,128)} %copy.148, f32[72,24,32]{2,1,0:T(8,128)S(1)} %copy.147), kind=kLoop, calls=%fused_computation.18 | loop fusion | flops 10616832 | bytes 15040512 | tf_op jit(solution)/shard_map/add | solution.py:103
  335.5 3.7 all-to-all-start.3
  339.2 28.5 %pad_maximum_fusion = f32[72,24,32,64]{3,2,1,0:T(8,128)} fusion(f32[72,24,32,32]{3,2,1,0:T(8,128)} %get-tuple-element.15, f32[72,24,32,32]{3,2,1,0:T(8,128)} %get-tuple-element.14), kind=kLoop, calls=%fused_computation.16 | loop fusion | flops 3538944 | bytes 28311552 | tf_op jit(solution)/shard_map/concatenate | solution.py:105
  367.7 24.3 %reshape.127 = f32[72,24,2048]{2,1,0:T(8,128)} reshape(f32[72,24,32,64]{3,2,1,0:T(8,128)} %pad_maximum_fusion) | data formatting | bytes 28311552 | tf_op jit(solution)/shard_map/reshape | solution.py:168
  392.7 40.0 %all_gather.7 = bf16[96,24,2,64]{1,0,3,2:T(8,128)(2,1)S(1)} all-gather(bf16[24,24,2,64]{1,0,3,2:T(8,128)(2,1)S(1)} %copy.93), channel_id=1, replica_groups=mesh['gx'=4,'gy'=8] {'gx'}, dimensions={0}, use_global_device_ids=true | all-gather | bytes 737280 | tf_op jit(solution)/shard_map/all_gather | solution.py:149
  432.7 5.8 %convolution_bitcast_fusion.14 = f32[96,4,2,64]{0,1,3,2:T(4,128)S(1)} fusion(bf16[96,24,2,64]{1,0,3,2:T(8,128)(2,1)S(1)} %all_gather.7, s32[24]{0:T(128)S(1)} %compare_select_fusion.2, s32[4]{0:T(128)S(1)} %iota_add_fusion), kind=kOutput, calls=%fused_computation.42 | convolution fusion | flops 14157120 | bytes 786544 | tf_op jit(solution)/shard_map/rkyc,xk->rxyc/dot_general | solution.py:43
  438.5 5.8 %convolution_bitcast_fusion.15 = f32[96,4,2,64]{0,1,3,2:T(4,128)S(1)} fusion(bf16[96,24,2,64]{1,0,3,2:T(8,128)(2,1)S(1)} %all_gather.7, s32[24]{0:T(128)S(1)} %compare_select_fusion.2, s32[4]{0:T(128)S(1)} %iota_add_fusion), kind=kOutput, calls=%fused_computation.43 | convolution fusion | flops 14157120 | bytes 786544 | tf_op jit(solution)/shard_map/rkyc,xk->rxyc/dot_general | solution.py:42
  (99 shorter events, 50.8 us)
Async XLA Ops:
  7.2 19.3 %copy-start = (bf16[4,2,32,512]{3,2,1,0:T(8,128)(2,1)S(1)}, bf16[4,2,32,512]{3,2,1,0:T(8,128)(2,1)}, u32[]{:S(2)}) copy-start(bf16[4,2,32,512]{3,2,1,0:T(8,128)(2,1)} %param.4) | copy-start | bytes 786436
  7.2 57.3 %reduce-scatter.3.cloned.1.call-start = ((), (), s32[]{:S(2)}) async-start(), calls=%async_computation.6 | async-start | bytes 1474560 | tf_op jit(solution)/shard_map/reduce_scatter | solution.py:130
  66.7 26.0 %all-to-all-start = ((bf16[8,2,4608]{2,1,0:T(2,128)(2,1)}), bf16[8,2,4608]{2,1,0:T(2,128)(2,1)S(1)}, u32[]{:S(2)}, u32[]{:S(2)}) async-start(bf16[8,2,4608]{2,1,0:T(2,128)(2,1)} %reshape.154), calls=%async_computation.1 | async-start | bytes 294912 | tf_op jit(solution)/shard_map/all_to_all | solution.py:139
  71.3 172.7 %reduce-scatter.5.cloned.1.call-start = ((), (), s32[]{:S(2)}) async-start(), calls=%async_computation.7 | async-start | bytes 1474560 | tf_op jit(solution)/shard_map/reduce_scatter | solution.py:130
  129.6 78.4 %copy-start.3 = (f32[512,96,1,1]{0,1,2,3:T(8,128)S(1)}, f32[512,96,1,1]{0,1,2,3:T(8,128)}, u32[]{:S(2)}) copy-start(f32[512,96,1,1]{0,1,2,3:T(8,128)} %reshape.128) | copy-start | bytes 589828
  129.7 78.8 %copy-start.2 = (f32[512,96,1,1]{0,1,2,3:T(8,128)S(1)}, f32[512,96,1,1]{0,1,2,3:T(8,128)}, u32[]{:S(2)}) copy-start(f32[512,96,1,1]{0,1,2,3:T(8,128)} %reshape.129) | copy-start | bytes 589828
  129.7 79.2 %copy-start.6 = (bf16[32,32]{1,0:T(8,128)(2,1)S(1)}, bf16[32,32]{1,0:T(8,128)(2,1)}, u32[]{:S(2)}) copy-start(bf16[32,32]{1,0:T(8,128)(2,1)} %param.6) | copy-start | bytes 6148
  211.2 3.0 copy-start.4
  335.5 56.5 %all-to-all-start.3 = ((bf16[72,16,64]{0,2,1:T(8,128)(2,1)}), bf16[72,16,64]{0,2,1:T(8,128)(2,1)S(1)}, u32[]{:S(2)}, u32[]{:S(2)}) async-start(bf16[72,16,64]{0,2,1:T(8,128)(2,1)} %copy.91), calls=%async_computation.5 | async-start | bytes 524288 | tf_op jit(solution)/shard_map/all_to_all | solution.py:144
  367.7 78.6 %copy-start.1 = (bf16[4,2,32,512]{3,2,1,0:T(8,128)(2,1)S(1)}, bf16[4,2,32,512]{3,2,1,0:T(8,128)(2,1)}, u32[]{:S(2)}) copy-start(bf16[4,2,32,512]{3,2,1,0:T(8,128)(2,1)} %param.4) | copy-start | bytes 786436
  392.0 53.4 %copy-start.5 = (bf16[4,2,32,512]{3,2,1,0:T(8,128)(2,1)S(1)}, bf16[4,2,32,512]{3,2,1,0:T(8,128)(2,1)}, u32[]{:S(2)}) copy-start(bf16[4,2,32,512]{3,2,1,0:T(8,128)(2,1)} %copy-done.4) | copy-start | bytes 786436
Sparse Core Ops, SparseCore 0:
  33.2 31.2 reduce-scatter.2
  216.2 27.7 reduce-scatter.4
where the time goes:
time: 463 us; the launch traced here: 454 us
  other arithmetic  141 us (30%)
  blocking collectives  104 us (22%)
  local copies, waits for them, and re-layouts  84.9 us (18%)
  waiting for transfers between devices  59.4 us (13%)
  matrix products  40.2 us (9%)
  between operations  15 us (3%)
  starting transfers between devices  8.86 us (2%)
    all_gather x2, blocking collectives, to_space(): lax.all_gather(returned, 'gx', axis=0, tiled=True).astype(jnp.float32)  78.1 us
    unnamed x2, other arithmetic  73 us
    reduce_scatter x2, waiting for transfers between devices, to_modes(): lax.psum_scatter(rotate(depth_spec.astype(jnp.float32), local_x[0], local...  59.3 us
    concatenate x1, other arithmetic, weight_grad(): return jnp.concatenate([real_part, imag_part], -1)  28.5 us
    reshape x1, local copies, waits for them, and re-layouts, per_device(): weight_grad(spectra_in, spectra_back)  24.3 us
    reshape x1, local copies, waits for them, and re-layouts, per_device(): spectral_weight.reshape(mode_rows, mode_cols, channels, 2 * channels)  20.8 us
    add x1, other arithmetic, weight_grad(): partial_outer(real_in, real_back) + partial_outer(imag_in, imag_back)  20 us
    dot_general x8, matrix products, rotate(): jnp.einsum(pattern, spectra, cosine_table, precision=lax.Precision.HIGHEST)  16 us
  transfers between devices with their start and end apart: 4, of which 2 were waited for; matrix products, arithmetic and copies ran while one was open for 16% of the time, Pallas kernels for 0%

commit v1 on v0

--- a/solution.py
+++ b/solution.py
@@ -10,6 +10,13 @@
 KY = 24
 KZ = 12
 KT = 8
+
+
+def trade_parts(x, name, split, join):
+    size = lax.axis_size(name)
+    shards = jnp.stack(jnp.split(x, size, axis=split), axis=0)
+    shards = lax.all_to_all(shards, name, split_axis=0, concat_axis=0)
+    return jnp.concatenate(shards, axis=join)
 
 
 def kept_angles(positions, kept_count, length):
@@ -141,7 +148,7 @@
 
     def to_space(spectra, factor):
         back_rows = settle(rotate(spectra, whole_y[0], whole_y[1], "mkc,yk->myc", -1.0))
-        returned = lax.all_to_all(back_rows, "gy", split_axis=1, concat_axis=0, tiled=True)
+        returned = trade_parts(back_rows, "gy", 1, 0)
         share = returned.shape[0] // KX
         returned = returned.reshape(share, KX, rows_y, 2 * channels)
         back_depth = settle(

time: 463 us -> 467 us (level)
  local copies, waits for them, and re-layouts: 84.9 us -> 89.6 us
    unnamed x22 -> x36, local copies, waits for them, and re-layouts: 5.86 us -> 10.7 us
where the time goes in v1:
time: 467 us; the launch traced here: 458 us
  other arithmetic  141 us (30%)
  blocking collectives  104 us (22%)
  local copies, waits for them, and re-layouts  89.6 us (19%)
  waiting for transfers between devices  59.4 us (13%)
  matrix products  40.2 us (9%)
  between operations  15 us (3%)
  starting transfers between devices  8.86 us (2%)
    all_gather x2, blocking collectives, to_space(): lax.all_gather(returned, 'gx', axis=0, tiled=True).astype(jnp.float32)  78.1 us
    unnamed x2, other arithmetic  73 us
    reduce_scatter x2, waiting for transfers between devices, to_modes(): lax.psum_scatter(rotate(depth_spec.astype(jnp.float32), local_x[0], local...  59.3 us
    concatenate x1, other arithmetic, weight_grad(): return jnp.concatenate([real_part, imag_part], -1)  28.5 us
    reshape x1, local copies, waits for them, and re-layouts, per_device(): weight_grad(spectra_in, spectra_back)  24.3 us
    reshape x1, local copies, waits for them, and re-layouts, per_device(): spectral_weight.reshape(mode_rows, mode_cols, channels, 2 * channels)  20.8 us
    add x1, other arithmetic, weight_grad(): partial_outer(real_in, real_back) + partial_outer(imag_in, imag_back)  20 us
    dot_general x8, matrix products, rotate(): jnp.einsum(pattern, spectra, cosine_table, precision=lax.Precision.HIGHEST)  16 us
  transfers between devices with their start and end apart: 4, of which 2 were waited for; matrix products, arithmetic and copies ran while one was open for 16% of the time, Pallas kernels for 0%

profile of v1, /device:TPU:0, one launch (start us, length us, event | category | flops | bytes accessed | tf_op | source)
XLA Modules:
  0.0 458.3 jit_solution(5512247143777212666)
XLA Ops:
  7.4 12.3 %add_sine_fusion = (f32[64,8,12,8]{1,0,3,2:T(8,128)}, f32[64,8,12,8]{1,0,3,2:T(8,128)S(1)}) fusion(f32[8,8]{0,1:T(8,128)S(1)} %fusion.94, f32[64,12]{0,1:T(8,128)S(1)} %fusion.75), kind=kLoop, calls=%fused_computation.19 | loop fusion | flops 49152 | bytes 396544 | tf_op jit(solution)/shard_map/sin | solution.py:40
  19.8 3.9 reshape.119
  23.7 2.8 reshape.118
  33.1 31.4 %reduce-scatter.3.cloned.1.call-done = bf16[24,24,2,64]{3,1,2,0:T(8,128)(2,1)} async-done(((bf16[96,24,2,64]{3,1,2,0:T(8,128)(2,1)}), bf16[24,24,2,64]{3,1,2,0:T(8,128)(2,1)}) %reduce-scatter.3.cloned.1.call-update) | async-done | bytes 147472 | tf_op jit(solution)/shard_map/reduce_scatter | solution.py:137
  66.7 4.6 %all-to-all-start = ((bf16[8,2,4608]{2,1,0:T(2,128)(2,1)}), bf16[8,2,4608]{2,1,0:T(2,128)(2,1)S(1)}, u32[]{:S(2)}, u32[]{:S(2)}) async-start(bf16[8,2,4608]{2,1,0:T(2,128)(2,1)} %reshape.144), calls=%async_computation.1 | async-start | bytes 294912 | tf_op jit(solution)/shard_map/all_to_all | solution.py:146
  71.8 20.8 %reshape.115 = bf16[72,24,32,64]{3,2,1,0:T(8,128)(2,1)} reshape(bf16[72,24,2048]{2,1,0:T(8,128)(2,1)} %param.7) | data formatting | bytes 14155776 | tf_op jit(solution)/shard_map/reshape | solution.py:122
  95.3 34.3 %fusion.2 = (f32[72,24,32]{2,1,0:T(8,128)}, f32[72,24,32]{2,1,0:T(8,128)}, f32[72,24,32]{2,1,0:T(8,128)}, f32[72,24,32]{2,1,0:T(8,128)S(1)}) fusion(f32[72,24,32]{2,1,0:T(8,128)S(1)} %copy.115, bf16[72,24,32,64]{3,2,1,0:T(8,128)(2,1)} %reshape.115, f32[72,24,32]{2,1,0:T(8,128)S(1)} %copy.114), kind=kLoop, calls=%fused_computation.10 | loop fusion | flops 17473536 | bytes 8404992
  129.7 2.3 copy.80
  141.5 14.6 %all_to_all.46 = bf16[8,72,2,64]{1,2,3,0:T(2,128)(2,1)S(1)} all-to-all(bf16[8,72,2,64]{1,2,3,0:T(2,128)(2,1)S(1)} %constant_dynamic-update-slice_fusion), channel_id=1, replica_groups=mesh['gx'=4,'gy'=8] {'gy'}, dimensions={0} | all-to-all | bytes 294912 | tf_op jit(solution)/shard_map/all_to_all | solution.py:18
  158.3 38.1 %all_gather.6 = bf16[96,24,2,64]{1,0,3,2:T(8,128)(2,1)S(1)} all-gather(bf16[24,24,2,64]{1,0,3,2:T(8,128)(2,1)S(1)} %copy.50), channel_id=1, replica_groups=mesh['gx'=4,'gy'=8] {'gx'}, dimensions={0}, use_global_device_ids=true | all-gather | bytes 737280 | tf_op jit(solution)/shard_map/all_gather | solution.py:156
  196.4 5.8 %convolution_bitcast_fusion.16 = f32[96,4,2,64]{0,1,3,2:T(4,128)S(1)} fusion(bf16[96,24,2,64]{1,0,3,2:T(8,128)(2,1)S(1)} %all_gather.6, s32[24]{0:T(128)S(1)} %compare_select_fusion.2, s32[4]{0:T(128)S(1)} %iota_add_fusion), kind=kOutput, calls=%fused_computation.44 | convolution fusion | flops 14157120 | bytes 786544 | tf_op jit(solution)/shard_map/rkyc,xk->rxyc/dot_general | solution.py:50
  202.2 5.8 %convolution_bitcast_fusion.17 = f32[96,4,2,64]{0,1,3,2:T(4,128)S(1)} fusion(bf16[96,24,2,64]{1,0,3,2:T(8,128)(2,1)S(1)} %all_gather.6, s32[24]{0:T(128)S(1)} %compare_select_fusion.2, s32[4]{0:T(128)S(1)} %iota_add_fusion), kind=kOutput, calls=%fused_computation.45 | convolution fusion | flops 14157120 | bytes 786544 | tf_op jit(solution)/shard_map/rkyc,xk->rxyc/dot_general | solution.py:49
  209.2 2.4 fusion.22
  216.4 27.9 %reduce-scatter.5.cloned.1.call-done = bf16[24,24,2,64]{3,1,2,0:T(8,128)(2,1)} async-done(((bf16[96,24,2,64]{3,1,2,0:T(8,128)(2,1)}), bf16[24,24,2,64]{3,1,2,0:T(8,128)(2,1)}) %reduce-scatter.5.cloned.1.call-update) | async-done | bytes 147472 | tf_op jit(solution)/shard_map/reduce_scatter | solution.py:137
  245.8 11.6 %all_to_all.47 = bf16[8,2,4608]{2,1,0:T(2,128)(2,1)S(1)} all-to-all(bf16[8,2,4608]{2,1,0:T(2,128)(2,1)S(1)} %reshape.146), channel_id=1, replica_groups=mesh['gx'=4,'gy'=8] {'gy'}, dimensions={0} | all-to-all | bytes 294912 | tf_op jit(solution)/shard_map/all_to_all | solution.py:146
  261.6 2.3 copy.117
  263.9 38.7 %fusion.6 = (f32[72,24,32]{2,1,0:T(8,128)}, f32[72,24,32]{2,1,0:T(8,128)}, f32[72,24,32]{2,1,0:T(8,128)}, f32[72,24,32]{2,1,0:T(8,128)}) fusion(f32[72,24,32]{2,1,0:T(8,128)} %copy.117, bf16[72,24,32,64]{3,2,1,0:T(8,128)(2,1)} %reshape.115, f32[72,24,32]{2,1,0:T(8,128)S(1)} %copy.116), kind=kLoop, calls=%fused_computation.14 | loop fusion | flops 17473536 | bytes 8404992
  314.9 20.0 %multiply_add_fusion = (f32[72,24,32,32]{3,2,1,0:T(8,128)}, f32[72,24,32,32]{3,2,1,0:T(8,128)}) fusion(f32[72,24,32]{2,1,0:T(8,128)S(1)} %copy.115, f32[72,24,32]{2,1,0:T(8,128)S(1)} %copy.114, f32[72,24,32]{2,1,0:T(8,128)} %copy.117, f32[72,24,32]{2,1,0:T(8,128)S(1)} %copy.116), kind=kLoop, calls=%fused_computation.18 | loop fusion | flops 10616832 | bytes 15040512 | tf_op jit(solution)/shard_map/add | solution.py:110
  340.2 3.7 all-to-all-start.3
  343.9 28.5 %pad_maximum_fusion = f32[72,24,32,64]{3,2,1,0:T(8,128)} fusion(f32[72,24,32,32]{3,2,1,0:T(8,128)} %get-tuple-element.15, f32[72,24,32,32]{3,2,1,0:T(8,128)} %get-tuple-element.14), kind=kLoop, calls=%fused_computation.16 | loop fusion | flops 3538944 | bytes 28311552 | tf_op jit(solution)/shard_map/concatenate | solution.py:112
  372.4 24.3 %reshape.117 = f32[72,24,2048]{2,1,0:T(8,128)} reshape(f32[72,24,32,64]{3,2,1,0:T(8,128)} %pad_maximum_fusion) | data formatting | bytes 28311552 | tf_op jit(solution)/shard_map/reshape | solution.py:175
  397.4 40.0 %all_gather.7 = bf16[96,24,2,64]{1,0,3,2:T(8,128)(2,1)S(1)} all-gather(bf16[24,24,2,64]{1,0,3,2:T(8,128)(2,1)S(1)} %copy.62), channel_id=1, replica_groups=mesh['gx'=4,'gy'=8] {'gx'}, dimensions={0}, use_global_device_ids=true | all-gather | bytes 737280 | tf_op jit(solution)/shard_map/all_gather | solution.py:156
  437.4 5.8 %convolution_bitcast_fusion.14 = f32[96,4,2,64]{0,1,3,2:T(4,128)S(1)} fusion(bf16[96,24,2,64]{1,0,3,2:T(8,128)(2,1)S(1)} %all_gather.7, s32[24]{0:T(128)S(1)} %compare_select_fusion.2, s32[4]{0:T(128)S(1)} %iota_add_fusion), kind=kOutput, calls=%fused_computation.42 | convolution fusion | flops 14157120 | bytes 786544 | tf_op jit(solution)/shard_map/rkyc,xk->rxyc/dot_general | solution.py:50
  443.2 5.8 %convolution_bitcast_fusion.15 = f32[96,4,2,64]{0,1,3,2:T(4,128)S(1)} fusion(bf16[96,24,2,64]{1,0,3,2:T(8,128)(2,1)S(1)} %all_gather.7, s32[24]{0:T(128)S(1)} %compare_select_fusion.2, s32[4]{0:T(128)S(1)} %iota_add_fusion), kind=kOutput, calls=%fused_computation.43 | convolution fusion | flops 14157120 | bytes 786544 | tf_op jit(solution)/shard_map/rkyc,xk->rxyc/dot_general | solution.py:49
  (113 shorter events, 55.5 us)
Async XLA Ops:
  7.2 19.3 %copy-start = (bf16[4,2,32,512]{3,2,1,0:T(8,128)(2,1)S(1)}, bf16[4,2,32,512]{3,2,1,0:T(8,128)(2,1)}, u32[]{:S(2)}) copy-start(bf16[4,2,32,512]{3,2,1,0:T(8,128)(2,1)} %param.4) | copy-start | bytes 786436
  7.2 57.3 %reduce-scatter.3.cloned.1.call-start = ((), (), s32[]{:S(2)}) async-start(), calls=%async_computation.6 | async-start | bytes 1474560 | tf_op jit(solution)/shard_map/reduce_scatter | solution.py:137
  66.7 26.0 %all-to-all-start = ((bf16[8,2,4608]{2,1,0:T(2,128)(2,1)}), bf16[8,2,4608]{2,1,0:T(2,128)(2,1)S(1)}, u32[]{:S(2)}, u32[]{:S(2)}) async-start(bf16[8,2,4608]{2,1,0:T(2,128)(2,1)} %reshape.144), calls=%async_computation.1 | async-start | bytes 294912 | tf_op jit(solution)/shard_map/all_to_all | solution.py:146
  71.3 173.1 %reduce-scatter.5.cloned.1.call-start = ((), (), s32[]{:S(2)}) async-start(), calls=%async_computation.7 | async-start | bytes 1474560 | tf_op jit(solution)/shard_map/reduce_scatter | solution.py:137
  129.6 78.7 %copy-start.3 = (f32[512,96,1,1]{0,1,2,3:T(8,128)S(1)}, f32[512,96,1,1]{0,1,2,3:T(8,128)}, u32[]{:S(2)}) copy-start(f32[512,96,1,1]{0,1,2,3:T(8,128)} %reshape.118) | copy-start | bytes 589828
  129.7 79.1 %copy-start.2 = (f32[512,96,1,1]{0,1,2,3:T(8,128)S(1)}, f32[512,96,1,1]{0,1,2,3:T(8,128)}, u32[]{:S(2)}) copy-start(f32[512,96,1,1]{0,1,2,3:T(8,128)} %reshape.119) | copy-start | bytes 589828
  129.7 79.5 %copy-start.6 = (bf16[32,32]{1,0:T(8,128)(2,1)S(1)}, bf16[32,32]{1,0:T(8,128)(2,1)}, u32[]{:S(2)}) copy-start(bf16[32,32]{1,0:T(8,128)(2,1)} %param.6) | copy-start | bytes 6148
  211.6 3.0 copy-start.4
  340.2 56.5 %all-to-all-start.3 = ((bf16[8,72,2,64]{1,2,3,0:T(2,128)(2,1)}), bf16[8,72,2,64]{1,2,3,0:T(2,128)(2,1)S(1)}, u32[]{:S(2)}, u32[]{:S(2)}) async-start(bf16[8,72,2,64]{1,2,3,0:T(2,128)(2,1)} %constant_dynamic-update-slice_fusion.8), calls=%async_computation.5 | async-start | bytes 524288 | tf_op jit(solution)/shard_map/all_to_all | solution.py:18
  372.4 78.6 %copy-start.1 = (bf16[4,2,32,512]{3,2,1,0:T(8,128)(2,1)S(1)}, bf16[4,2,32,512]{3,2,1,0:T(8,128)(2,1)}, u32[]{:S(2)}) copy-start(bf16[4,2,32,512]{3,2,1,0:T(8,128)(2,1)} %param.4) | copy-start | bytes 786436
  396.8 53.4 %copy-start.5 = (bf16[4,2,32,512]{3,2,1,0:T(8,128)(2,1)S(1)}, bf16[4,2,32,512]{3,2,1,0:T(8,128)(2,1)}, u32[]{:S(2)}) copy-start(bf16[4,2,32,512]{3,2,1,0:T(8,128)(2,1)} %copy-done.4) | copy-start | bytes 786436
Sparse Core Ops, SparseCore 0:
  33.2 31.2 reduce-scatter.2
  216.5 27.7 reduce-scatter.4
